TPU v7x, 32 devices: a whole 2x2x4 slice. The times are simulated.
32 devices in a mesh: view: 2 (over y), row: 2 (over x), col: 8 (over z, core).
Axes of the slice: x: 2, y: 2, z: 4, core: 2. Of those that a mesh axis runs over, the one named last changes fastest.
Arguments:
- inputs: bfloat16 [2, 512, 8192], P('view', 'col', 'row'), may hold values from -28 to 28, as said below
- weight: bfloat16 [8192, 8192], P('row', 'col'), may hold values from -0.0625 to 0.0625
Outputs:
- grad_hidden: bfloat16 [2, 512, 8192], P('view', 'col', 'row')
- grad_weight: float32 [8192, 8192], P('row', 'col')
Inputs may be any that keep to these rules, and one draw needn't show every extreme that they name: `inputs`: feature activations of the two views of a clip; each feature has its own scale.
All inputs are finite; a program needn't handle non-finite values.
Results may differ from a plain program's by a relative error of at most 0.025.
Values may be sent and summed in bfloat16 or wider, within the bound.
No kernel may reach another device: no remote copies, remote signals or barrier semaphores. Data moves between devices by JAX's collectives and lax.ppermute only.
A program may use at most 128 MiB of HBM per device.

v0:
```python
import math
import jax
import jax.numpy as jnp
from jax import lax
from jax.sharding import PartitionSpec as P

off_weight = 0.0051
norm_eps = 1e-05


def from_partner(block, axis, distance):
    count = lax.axis_size(axis)
    route = []
    for low in range(count):
        high = low | 1 << distance
        if high != low and high < count:
            route += [(low, high), (high, low)]
    return lax.ppermute(block, axis, route)


def shards(inputs, weight):
    hidden = lax.all_gather(inputs[0], "col", axis=0, tiled=True)
    batch = hidden.shape[0]
    columns = weight
    pre = lax.psum_scatter(
        lax.dot_general(
            columns, hidden, (((0,), (1,)), ((), ())), preferred_element_type=jnp.float32
        ).astype(jnp.bfloat16),
        "row",
        scatter_dimension=0,
        tiled=True,
    ).astype(jnp.float32)
    centred = pre - jnp.mean(pre, axis=1, keepdims=True)
    rstd = lax.rsqrt(jnp.mean(centred * centred, axis=1, keepdims=True) + norm_eps)
    own = (centred * rstd).astype(jnp.bfloat16)
    partner = from_partner(own, "view", 0)
    own_f = own.astype(jnp.float32)
    partner_f = partner.astype(jnp.float32)
    diag = jnp.sum(own_f * partner_f, axis=1, keepdims=True) / batch
    piece = lax.all_gather(partner, ("row", "col"), axis=0, tiled=True)
    corr = (
        lax.dot_general(own, piece, (((1,), (1,)), ((), ())), preferred_element_type=jnp.float32)
        / batch
    )
    mixed = jnp.dot(corr.astype(jnp.bfloat16), piece, preferred_element_type=jnp.float32)
    scale_diag = 2.0 * (diag - 1.0) - 2.0 * off_weight * diag
    dnorm = 2.0 * off_weight * mixed + scale_diag * partner_f
    inner = jnp.mean(dnorm * own_f, axis=1, keepdims=True)
    dpre = (rstd * (dnorm - jnp.mean(dnorm, axis=1, keepdims=True) - own_f * inner)).astype(
        jnp.bfloat16
    )
    grads = lax.all_gather(dpre, "row", axis=0, tiled=True)
    local_weight = lax.dot_general(
        hidden, grads, (((0,), (1,)), ((), ())), preferred_element_type=jnp.float32
    )
    grad_weight = lax.psum(local_weight.astype(jnp.bfloat16), "view").astype(
        jnp.float32
    ) / math.sqrt(2.0 * batch)
    columns = grads
    grad_hidden = lax.psum_scatter(
        lax.dot_general(
            columns, weight, (((0,), (1,)), ((), ())), preferred_element_type=jnp.float32
        ).astype(jnp.bfloat16),
        "col",
        scatter_dimension=0,
        tiled=True,
    )
    return (grad_hidden[None], grad_weight)


def solution(mesh):
    return jax.shard_map(
        shards,
        mesh=mesh,
        in_specs=(P("view", "col", "row"), P("row", "col")),
        out_specs=(P("view", "col", "row"), P("row", "col")),
        check_vma=False,
    )
```

profile of v0, /device:TPU:0, one launch (start us, length us, event | category | flops | bytes accessed | tf_op | source)
XLA Modules:
  0.0 486.3 jit_solution(11138176716313369393)
XLA Ops:
  7.2 0.0 all-gather.9.cloned.1.call-start
  7.2 0.7 all-gather.9.cloned.1.call-update
  7.9 0.0 reduce-scatter.3.cloned.1.call-start
  7.9 51.2 %all-gather.9.cloned.1.call-done = bf16[1,512,4096]{2,1,0:T(8,128)(2,1)} async-done(((bf16[1,64,4096]{2,1,0:T(8,128)(2,1)}), bf16[1,512,4096]{2,1,0:T(8,128)(2,1)}) %all-gather.9.cloned.1.call-update) | async-done | bytes 4194320 | tf_op jit(solution)/shard_map/all_gather | solution.py:22
  59.2 10.1 %fusion.4 = bf16[1024,512]{1,0:T(8,128)(2,1)} fusion(bf16[4096,1024]{1,0:T(8,128)(2,1)} %param.3, bf16[1,512,4096]{2,1,0:T(8,128)(2,1)} %all-gather.9.cloned.1.call-done), kind=kOutput, calls=%fused_computation.11 | convolution fusion | flops 4295491584 | bytes 13631488 | tf_op jit(solution)/shard_map/dot_general | solution.py:26
  69.3 0.0 reduce-scatter.3.cloned.1.call-update
  69.3 0.0 all-gather.5.cloned.1.call-start
  69.4 19.3 %reduce-scatter.3.cloned.1.call-done = bf16[512,512]{1,0:T(8,128)(2,1)} async-done(((bf16[1024,512]{1,0:T(8,128)(2,1)}), bf16[512,512]{1,0:T(8,128)(2,1)}) %reduce-scatter.3.cloned.1.call-update) | async-done | bytes 524304 | tf_op jit(solution)/shard_map/reduce_scatter | solution.py:25
  88.7 1.2 convert_reduce_fusion
  89.9 1.3 fusion.11
  91.2 1.3 fusion.12
  92.5 1.5 collective-permute-start
  94.0 12.0 %collective-permute-done = bf16[512,512]{1,0:T(8,128)(2,1)S(1)} collective-permute-done((bf16[512,512]{1,0:T(8,128)(2,1)S(1)}, bf16[512,512]{1,0:T(8,128)(2,1)S(1)}, u32[]{:S(2)}, u32[]{:S(2)}) %collective-permute-start) | collective-permute-done | bytes 524320 | tf_op jit(solution)/shard_map/ppermute | solution.py:18
  106.0 0.8 copy-done.1
  106.8 0.0 all-gather.5.cloned.1.call-update
  106.8 0.0 all-gather.7.cloned.1.call-start
  106.9 1.6 fusion.13
  108.6 72.7 %all-gather.5.cloned.1.call-done = bf16[8192,512]{1,0:T(8,128)(2,1)} async-done(((bf16[512,512]{1,0:T(8,128)(2,1)}), bf16[8192,512]{1,0:T(8,128)(2,1)}) %all-gather.5.cloned.1.call-update) | async-done | bytes 8388624 | tf_op jit(solution)/shard_map/all_gather | solution.py:40
  181.3 15.2 %fusion.19 = (f32[512]{0:T(512)S(1)}, f32[512]{0:T(512)S(1)}, f32[512,512]{1,0:T(8,128)S(1)}) fusion(bf16[512,512]{1,0:T(8,128)(2,1)S(1)} %fusion.12, bf16[512,512]{1,0:T(8,128)(2,1)} %copy-done.1, f32[512]{0:T(512)S(1)} %multiply_subtract_fusion, bf16[8192,512]{1,0:T(8,128)(2,1)} %all-gather.5.cloned.1.call-done), kind=kOutput, calls=%fused_computation.32 | convolution fusion | flops 8600420352 | bytes 10491904 | tf_op jit(solution)/shard_map/dot_general | solution.py:45
  196.6 1.1 fusion.17
  197.7 0.2 all-reduce.2.cloned.1.call-start
  197.9 19.8 %all-gather.7.cloned.1.call-done = bf16[1024,512]{1,0:T(8,128)(2,1)} async-done(((bf16[512,512]{1,0:T(8,128)(2,1)}), bf16[1024,512]{1,0:T(8,128)(2,1)}) %all-gather.7.cloned.1.call-update) | async-done | bytes 1048592 | tf_op jit(solution)/shard_map/all_gather | solution.py:52
  217.7 10.4 %convert_bitcast_fusion = bf16[4096,1024]{0,1:T(8,128)(2,1)} fusion(bf16[1024,512]{1,0:T(8,128)(2,1)} %all-gather.7.cloned.1.call-done, bf16[1,512,4096]{2,1,0:T(8,128)(2,1)} %all-gather.9.cloned.1.call-done), kind=kOutput, calls=%fused_computation.2 | convolution fusion | flops 4299161600 | bytes 13631488 | tf_op jit(solution)/shard_map/dot_general | solution.py:53
  228.2 0.0 all-reduce.2.cloned.1.call-update
  228.2 0.0 reduce-scatter.5.cloned.1.call-start
  228.2 1.1 copy-done.2
  229.4 9.6 %convolution_convert_fusion = bf16[512,4096]{1,0:T(8,128)(2,1)} fusion(bf16[1024,512]{1,0:T(8,128)(2,1)S(1)} %copy-done.2, bf16[4096,1024]{1,0:T(8,128)(2,1)} %param.3), kind=kOutput, calls=%fused_computation.3 | convolution fusion | flops 4297064448 | bytes 13631488 | tf_op jit(solution)/shard_map/dot_general | solution.py:61
  239.0 0.0 reduce-scatter.5.cloned.1.call-update
  239.0 187.4 %all-reduce.2.cloned.1.call-done = bf16[4096,1024]{0,1:T(8,128)(2,1)} async-done(((bf16[4096,1024]{0,1:T(8,128)(2,1)}), bf16[4096,1024]{0,1:T(8,128)(2,1)}) %all-reduce.2.cloned.1.call-update) | async-done | bytes 8388624 | tf_op jit(solution)/shard_map/psum | solution.py:56
  426.4 11.7 %convert_multiply_fusion = f32[4096,1024]{0,1:T(8,128)} fusion(bf16[4096,1024]{0,1:T(8,128)(2,1)} %all-reduce.2.cloned.1.call-done), kind=kLoop, calls=%fused_computation | loop fusion | flops 8388608 | bytes 25165824 | tf_op jit(solution)/shard_map/div | solution.py:56
  438.1 17.5 %copy.5 = f32[4096,1024]{1,0:T(8,128)} copy(f32[4096,1024]{0,1:T(8,128)} %convert_multiply_fusion) | data formatting | bytes 33554432
  455.6 23.8 %reduce-scatter.5.cloned.1.call-done = bf16[64,4096]{1,0:T(8,128)(2,1)} async-done(((bf16[512,4096]{1,0:T(8,128)(2,1)}), bf16[64,4096]{1,0:T(8,128)(2,1)}) %reduce-scatter.5.cloned.1.call-update) | async-done | bytes 524304 | tf_op jit(solution)/shard_map/reduce_scatter | solution.py:60
  (9 shorter events, 0.0 us)
Async XLA Ops:
  7.2 52.0 %all-gather.9.cloned.1.call-start = ((), (), s32[]{:S(2)}) async-start(), calls=%async_computation.7 | async-start | bytes 4718592 | tf_op jit(solution)/shard_map/all_gather | solution.py:22
  7.9 80.8 %reduce-scatter.3.cloned.1.call-start = ((), (), s32[]{:S(2)}) async-start(), calls=%async_computation.2 | async-start | bytes 1572864 | tf_op jit(solution)/shard_map/reduce_scatter | solution.py:25
  69.3 112.0 %all-gather.5.cloned.1.call-start = ((), (), s32[]{:S(2)}) async-start(), calls=%async_computation.3 | async-start | bytes 8912896 | tf_op jit(solution)/shard_map/all_gather | solution.py:40
  92.5 13.6 %collective-permute-start = (bf16[512,512]{1,0:T(8,128)(2,1)S(1)}, bf16[512,512]{1,0:T(8,128)(2,1)S(1)}, u32[]{:S(2)}, u32[]{:S(2)}) collective-permute-start(bf16[512,512]{1,0:T(8,128)(2,1)S(1)} %fusion.12), channel_id=1, source_target_pairs={{0,16},{16,0},{1,17},{17,1},{2,18},{18,2},{3,19},{19,3},{4,20},{20... | collective-permute-start | bytes 1572872 | tf_op jit(solution)/shard_map/ppermute | solution.py:18
  106.0 0.8 copy-start.1
  106.8 110.9 %all-gather.7.cloned.1.call-start = ((), (), s32[]{:S(2)}) async-start(), calls=%async_computation.4 | async-start | bytes 1572864 | tf_op jit(solution)/shard_map/all_gather | solution.py:52
  108.5 88.0 %copy-start = (bf16[512,512]{1,0:T(8,128)(2,1)S(1)}, bf16[512,512]{1,0:T(8,128)(2,1)}, u32[]{:S(2)}) copy-start(bf16[512,512]{1,0:T(8,128)(2,1)} %reduce-scatter.3.cloned.1.call-done) | copy-start | bytes 1572868
  197.7 228.7 %all-reduce.2.cloned.1.call-start = ((), (), s32[]{:S(2)}) async-start(), calls=%async_computation.6 | async-start | bytes 16777216 | tf_op jit(solution)/shard_map/psum | solution.py:56
  228.2 1.2 copy-start.2
  228.2 251.2 %reduce-scatter.5.cloned.1.call-start = ((), (), s32[]{:S(2)}) async-start(), calls=%async_computation.5 | async-start | bytes 4718592 | tf_op jit(solution)/shard_map/reduce_scatter | solution.py:60
Sparse Core Ops, SparseCore 0:
  9.6 49.5 all-gather.8
  69.4 19.1 reduce-scatter.2
  107.0 74.2 all-gather.4
  197.8 19.8 all-gather.6
  228.3 198.0 all-reduce.1
  429.1 50.2 reduce-scatter.4
where the time goes:
time: 487 us; the launch traced here: 486 us
  waiting for transfers between devices  387 us (79%)
  matrix products  45.4 us (9%)
  local copies, waits for them, and re-layouts  19.5 us (4%)
  other arithmetic  18.3 us (4%)
  between operations  14.2 us (3%)
    psum x1, waiting for transfers between devices, shards(): lax.psum(local_weight.astype(jnp.bfloat16), 'view').astype(jnp.float32)  187 us
    all_gather x1, waiting for transfers between devices, shards(): piece = lax.all_gather(partner, ('row', 'col'), axis=0, tiled=True)  72.7 us
    all_gather x1, waiting for transfers between devices, shards(): hidden = lax.all_gather(inputs[0], 'col', axis=0, tiled=True)  51.2 us
    reduce_scatter x1, waiting for transfers between devices, shards(): lax.psum_scatter(lax.dot_general(columns, weight, (((0,), (1,)), ((), ())...  23.8 us
    all_gather x1, waiting for transfers between devices, shards(): grads = lax.all_gather(dpre, 'row', axis=0, tiled=True)  19.8 us
    unnamed x7, local copies, waits for them, and re-layouts  19.5 us
    reduce_scatter x1, waiting for transfers between devices, shards(): lax.psum_scatter(lax.dot_general(columns, hidden, (((0,), (1,)), ((), ())...  19.3 us
    dot_general x1, matrix products, shards(): jnp.dot(corr.astype(jnp.bfloat16), piece, preferred_element_type=jnp.floa...  15.2 us
  transfers between devices with their start and end apart: 7, of which 7 were waited for; matrix products, arithmetic and copies ran while one was open for 8% of the time, Pallas kernels for 0%

commit v1 on v0

--- a/solution.py
+++ b/solution.py
@@ -1,3 +1,4 @@
+import functools
 import math
 import jax
 import jax.numpy as jnp
@@ -6,6 +7,14 @@
 
 off_weight = 0.0051
 norm_eps = 1e-05
+
+
+def sheet_pass(sample, link_axis):
+    piece_next = lax.all_gather(sample, link_axis)
+    return jnp.sum(piece_next, axis=0)
+
+
+store_the_pairs_all = functools.partial(sheet_pass, link_axis="view")
 
 
 def from_partner(block, axis, distance):
@@ -53,7 +62,7 @@
     local_weight = lax.dot_general(
         hidden, grads, (((0,), (1,)), ((), ())), preferred_element_type=jnp.float32
     )
-    grad_weight = lax.psum(local_weight.astype(jnp.bfloat16), "view").astype(
+    grad_weight = store_the_pairs_all(local_weight.astype(jnp.bfloat16)).astype(
         jnp.float32
     ) / math.sqrt(2.0 * batch)
     columns = grads

time: 487 us -> 539 us (1.11)
  other arithmetic: 18.3 us -> 65.3 us
  local copies, waits for them, and re-layouts: 19.5 us -> 47.2 us
  waiting for transfers between devices: 387 us -> 364 us
    all_gather x0 -> x1, waiting for transfers between devices: none -> 188 us  [sheet_pass(): piece_next = lax.all_gather(sample, link_axis)]
    psum x1 -> x0, waiting for transfers between devices: 187 us -> none  [shards(): lax.psum(local_weight.astype(jnp.bfloat16), 'view').astype(jnp.float32)]
    reduce_sum x0 -> x1, other arithmetic: none -> 47.2 us  [sheet_pass(): return jnp.sum(piece_next, axis=0)]
    all_gather x0 -> x1, local copies, waits for them, and re-layouts: none -> 27.8 us  [sheet_pass(): piece_next = lax.all_gather(sample, link_axis)]
    reduce_scatter x1, waiting for transfers between devices: 23.8 us -> 0.01 us  [shards(): lax.psum_scatter(lax.dot_general(columns, weight, (((0,), (1,)), ((), ())...]
  transfers between devices with their start and end apart: 7 -> 7, of which waited for: 7 -> 6; matrix products, arithmetic and copies ran while one was open for 8% -> 21% of each run, Pallas kernels for 0% -> 0%
where the time goes in v1:
time: 539 us; the launch traced here: 538 us
  waiting for transfers between devices  364 us (68%)
  other arithmetic  65.3 us (12%)
  local copies, waits for them, and re-layouts  47.2 us (9%)
  matrix products  45.7 us (8%)
  between operations  14.2 us (3%)
    all_gather x1, waiting for transfers between devices, sheet_pass(): piece_next = lax.all_gather(sample, link_axis)  188 us
    all_gather x1, waiting for transfers between devices, shards(): piece = lax.all_gather(partner, ('row', 'col'), axis=0, tiled=True)  72.7 us
    all_gather x1, waiting for transfers between devices, shards(): hidden = lax.all_gather(inputs[0], 'col', axis=0, tiled=True)  51.2 us
    reduce_sum x1, other arithmetic, sheet_pass(): return jnp.sum(piece_next, axis=0)  47.2 us
    all_gather x1, local copies, waits for them, and re-layouts, sheet_pass(): piece_next = lax.all_gather(sample, link_axis)  27.8 us
    all_gather x1, waiting for transfers between devices, shards(): grads = lax.all_gather(dpre, 'row', axis=0, tiled=True)  19.8 us
    unnamed x7, local copies, waits for them, and re-layouts  19.4 us
    reduce_scatter x1, waiting for transfers between devices, shards(): lax.psum_scatter(lax.dot_general(columns, hidden, (((0,), (1,)), ((), ())...  19.3 us
  transfers between devices with their start and end apart: 7, of which 6 were waited for; matrix products, arithmetic and copies ran while one was open for 21% of the time, Pallas kernels for 0%

profile of v1, /device:TPU:0, one launch (start us, length us, event | category | flops | bytes accessed | tf_op | source)
XLA Modules:
  0.0 538.0 jit_solution(6109151824123598792)
XLA Ops:
  7.2 0.0 all-gather.11.cloned.1.call-start
  7.2 0.7 all-gather.11.cloned.1.call-update
  7.9 0.0 reduce-scatter.3.cloned.1.call-start
  7.9 51.2 %all-gather.11.cloned.1.call-done = bf16[1,512,4096]{2,1,0:T(8,128)(2,1)} async-done(((bf16[1,64,4096]{2,1,0:T(8,128)(2,1)}), bf16[1,512,4096]{2,1,0:T(8,128)(2,1)}) %all-gather.11.cloned.1.call-update) | async-done | bytes 4194320 | tf_op jit(solution)/shard_map/all_gather | solution.py:31
  59.2 10.1 %fusion.4 = bf16[1024,512]{1,0:T(8,128)(2,1)} fusion(bf16[4096,1024]{1,0:T(8,128)(2,1)} %param.3, bf16[1,512,4096]{2,1,0:T(8,128)(2,1)} %all-gather.11.cloned.1.call-done), kind=kOutput, calls=%fused_computation.11 | convolution fusion | flops 4295491584 | bytes 13631488 | tf_op jit(solution)/shard_map/dot_general | solution.py:35
  69.3 0.0 reduce-scatter.3.cloned.1.call-update
  69.3 0.0 all-gather.7.cloned.1.call-start
  69.4 19.3 %reduce-scatter.3.cloned.1.call-done = bf16[512,512]{1,0:T(8,128)(2,1)} async-done(((bf16[1024,512]{1,0:T(8,128)(2,1)}), bf16[512,512]{1,0:T(8,128)(2,1)}) %reduce-scatter.3.cloned.1.call-update) | async-done | bytes 524304 | tf_op jit(solution)/shard_map/reduce_scatter | solution.py:34
  88.7 1.2 convert_reduce_fusion
  89.9 1.3 fusion.11
  91.2 1.3 fusion.12
  92.5 1.5 collective-permute-start
  94.0 12.0 %collective-permute-done = bf16[512,512]{1,0:T(8,128)(2,1)S(1)} collective-permute-done((bf16[512,512]{1,0:T(8,128)(2,1)S(1)}, bf16[512,512]{1,0:T(8,128)(2,1)S(1)}, u32[]{:S(2)}, u32[]{:S(2)}) %collective-permute-start) | collective-permute-done | bytes 524320 | tf_op jit(solution)/shard_map/ppermute | solution.py:27
  106.0 0.8 copy-done.1
  106.8 0.0 all-gather.7.cloned.1.call-update
  106.8 0.0 all-gather.9.cloned.1.call-start
  106.9 1.6 fusion.13
  108.6 72.7 %all-gather.7.cloned.1.call-done = bf16[8192,512]{1,0:T(8,128)(2,1)} async-done(((bf16[512,512]{1,0:T(8,128)(2,1)}), bf16[8192,512]{1,0:T(8,128)(2,1)}) %all-gather.7.cloned.1.call-update) | async-done | bytes 8388624 | tf_op jit(solution)/shard_map/all_gather | solution.py:49
  181.3 15.2 %fusion.19 = (f32[512]{0:T(512)S(1)}, f32[512]{0:T(512)S(1)}, f32[512,512]{1,0:T(8,128)S(1)}) fusion(bf16[512,512]{1,0:T(8,128)(2,1)S(1)} %fusion.12, bf16[512,512]{1,0:T(8,128)(2,1)} %copy-done.1, f32[512]{0:T(512)S(1)} %multiply_subtract_fusion, bf16[8192,512]{1,0:T(8,128)(2,1)} %all-gather.7.cloned.1.call-done), kind=kOutput, calls=%fused_computation.32 | convolution fusion | flops 8600420352 | bytes 10491904 | tf_op jit(solution)/shard_map/dot_general | solution.py:54
  196.5 1.1 fusion.17
  197.7 0.0 all-gather.9.cloned.1.call-update
  197.7 0.2 all-gather.13.cloned.1.call-start
  197.9 19.8 %all-gather.9.cloned.1.call-done = bf16[1024,512]{1,0:T(8,128)(2,1)} async-done(((bf16[512,512]{1,0:T(8,128)(2,1)}), bf16[1024,512]{1,0:T(8,128)(2,1)}) %all-gather.9.cloned.1.call-update) | async-done | bytes 1048592 | tf_op jit(solution)/shard_map/all_gather | solution.py:61
  217.7 10.4 %convert_bitcast_fusion = bf16[4096,1024]{0,1:T(8,128)(2,1)} fusion(bf16[1024,512]{1,0:T(8,128)(2,1)} %all-gather.9.cloned.1.call-done, bf16[1,512,4096]{2,1,0:T(8,128)(2,1)} %all-gather.11.cloned.1.call-done), kind=kOutput, calls=%fused_computation.2 | convolution fusion | flops 4299161600 | bytes 13631488 | tf_op jit(solution)/shard_map/dot_general | solution.py:62
  228.2 0.0 reduce-scatter.5.cloned.1.call-start
  228.2 1.1 copy-done.2
  229.4 9.9 %convolution_convert_fusion = bf16[512,4096]{1,0:T(8,128)(2,1)} fusion(bf16[1024,512]{1,0:T(8,128)(2,1)S(1)} %copy-done.2, bf16[4096,1024]{1,0:T(8,128)(2,1)} %param.3), kind=kOutput, calls=%fused_computation.3 | convolution fusion | flops 4297064448 | bytes 13631488 | tf_op jit(solution)/shard_map/dot_general | solution.py:70
  239.3 187.8 %all-gather.13.cloned.1.call-done = bf16[8192,1024]{0,1:T(8,128)(2,1)} async-done(((bf16[4096,1024]{0,1:T(8,128)(2,1)}), bf16[8192,1024]{0,1:T(8,128)(2,1)}) %all-gather.13.cloned.1.call-update) | async-done | bytes 16777232 | tf_op jit(solution)/shard_map/all_gather | solution.py:13
  427.2 27.8 %reshape.37 = bf16[2,4096,1024]{1,0,2:T(2,128)(2,1)} reshape(bf16[8192,1024]{0,1:T(8,128)(2,1)} %all-gather.13.cloned.1.call-done) | data formatting | bytes 33554432 | tf_op jit(solution)/shard_map/all_gather | solution.py:13
  455.0 47.2 %reduce_sum.62 = bf16[4096,1024]{0,1:T(8,128)(2,1)} reduce(bf16[2,4096,1024]{1,0,2:T(2,128)(2,1)} %reshape.37, bf16[]{:T(256)} %constant.26.clone.1), dimensions={0}, to_apply=%region_7.0 | reduce | flops 4194304 | bytes 25165826 | tf_op jit(solution)/shard_map/reduce_sum | solution.py:14
  502.2 11.5 %convert_multiply_fusion = f32[4096,1024]{0,1:T(8,128)} fusion(bf16[4096,1024]{0,1:T(8,128)(2,1)} %reduce_sum.62), kind=kLoop, calls=%fused_computation | loop fusion | flops 8388608 | bytes 25165824 | tf_op jit(solution)/shard_map/div | solution.py:65
  513.7 17.4 %copy.6 = f32[4096,1024]{1,0:T(8,128)} copy(f32[4096,1024]{0,1:T(8,128)} %convert_multiply_fusion) | data formatting | bytes 33554432
  (11 shorter events, 0.1 us)
Async XLA Ops:
  7.2 52.0 %all-gather.11.cloned.1.call-start = ((), (), s32[]{:S(2)}) async-start(), calls=%async_computation.6 | async-start | bytes 4718592 | tf_op jit(solution)/shard_map/all_gather | solution.py:31
  7.9 80.8 %reduce-scatter.3.cloned.1.call-start = ((), (), s32[]{:S(2)}) async-start(), calls=%async_computation.2 | async-start | bytes 1572864 | tf_op jit(solution)/shard_map/reduce_scatter | solution.py:34
  69.3 112.0 %all-gather.7.cloned.1.call-start = ((), (), s32[]{:S(2)}) async-start(), calls=%async_computation.3 | async-start | bytes 8912896 | tf_op jit(solution)/shard_map/all_gather | solution.py:49
  92.5 13.6 %collective-permute-start = (bf16[512,512]{1,0:T(8,128)(2,1)S(1)}, bf16[512,512]{1,0:T(8,128)(2,1)S(1)}, u32[]{:S(2)}, u32[]{:S(2)}) collective-permute-start(bf16[512,512]{1,0:T(8,128)(2,1)S(1)} %fusion.12), channel_id=1, source_target_pairs={{0,16},{16,0},{1,17},{17,1},{2,18},{18,2},{3,19},{19,3},{4,20},{20... | collective-permute-start | bytes 1572872 | tf_op jit(solution)/shard_map/ppermute | solution.py:27
  106.0 0.8 copy-start.1
  106.8 110.9 %all-gather.9.cloned.1.call-start = ((), (), s32[]{:S(2)}) async-start(), calls=%async_computation.4 | async-start | bytes 1572864 | tf_op jit(solution)/shard_map/all_gather | solution.py:61
  108.5 88.0 %copy-start = (bf16[512,512]{1,0:T(8,128)(2,1)S(1)}, bf16[512,512]{1,0:T(8,128)(2,1)}, u32[]{:S(2)}) copy-start(bf16[512,512]{1,0:T(8,128)(2,1)} %reduce-scatter.3.cloned.1.call-done) | copy-start | bytes 1572868
  197.7 229.5 %all-gather.13.cloned.1.call-start = ((), (), s32[]{:S(2)}) async-start(), calls=%async_computation.7 | async-start | bytes 25165824 | tf_op jit(solution)/shard_map/all_gather | solution.py:13
  228.2 1.2 copy-start.2
  228.2 302.9 %reduce-scatter.5.cloned.1.call-start = ((), (), s32[]{:S(2)}) async-start(), calls=%async_computation.5 | async-start | bytes 4718592 | tf_op jit(solution)/shard_map/reduce_scatter | solution.py:69
Sparse Core Ops, SparseCore 0:
  9.6 49.5 all-gather.10
  69.4 19.1 reduce-scatter.2
  107.0 74.2 all-gather.6
  197.8 19.8 all-gather.8
  228.3 198.8 all-gather.12
  429.9 49.8 reduce-scatter.4
